TPU v7x, 32 devices: a whole 2x2x4 slice. The times are simulated.
32 devices in a mesh: dp: 8 (over y, x, core), shard: 4 (over z).
Axes of the slice: x: 2, y: 2, z: 4, core: 2. Of those that a mesh axis runs over, the one named last changes fastest.
Arguments:
- activations: bfloat16 [4096, 4096], P('dp', 'shard'), may hold values from -6 to 6
- out_grads: bfloat16 [4096, 14336], P('dp', 'shard'), may hold values from -6 to 6
- sign_bits: int32 [14336], P('shard'), may hold values from 0 to 1
- block_ids: int32 [4, 8], replicated, may hold values from 0 to 111, as said below
Outputs:
- gram: float32 [4096, 1024], P('shard')
Inputs may be any that keep to these rules, and one draw needn't show every extreme that they name: `block_ids`: row o holds 4 runs of 2 entries; the entries of a run are distinct blocks of one shard s (ids s * 28 + 0 to s * 28 + 27), and the runs of a row come from distinct shards.
All inputs are finite; a program needn't handle non-finite values.
Results may differ from a plain program's by a relative error of at most 0.006.
Values may be sent and summed in bfloat16 or wider, within the bound.
A program may use at most 64 MiB of HBM per device.

v0:
```python
import math
import jax
import jax.numpy as jnp
from jax import lax
from jax.sharding import PartitionSpec as P

BLK = 128
CAP = 2


def partner_2(x, axis, distance):
    return lax.ppermute(x, axis, [(i, i ^ 1 << distance) for i in range(lax.axis_size(axis))])


def parity_table(count):
    index = jnp.arange(count, dtype=jnp.int32)
    total = jnp.zeros((count, count), jnp.int32)
    for level in range(count.bit_length() - 1):
        total = total + (
            jnp.right_shift(index[:, None], level) & jnp.right_shift(index[None, :], level) & 1
        )
    return (1 - 2 * (total % 2)).astype(jnp.float32)


def route_sampled(mixed, block_ids, me_index, shards, blocks_per, tokens, width):
    groups = block_ids.shape[1] // CAP
    sources = block_ids[:, ::CAP] // blocks_per
    local_ids = (block_ids % blocks_per).reshape(shards, groups, CAP)
    matched = sources == me_index
    chosen = jnp.sum(jnp.where(matched[:, :, None], local_ids, 0), axis=1)
    live_rows = jnp.any(matched, axis=1).astype(jnp.bfloat16)
    outgoing = jnp.take(mixed, chosen.reshape(-1), axis=0).reshape(shards, CAP, tokens, width)
    return (outgoing * live_rows[:, None, None, None], jnp.take(sources, me_index, axis=0))


def body(activations, out_grads, sign_bits, block_ids):
    shards = lax.axis_size("shard")
    me_index = lax.axis_index("shard")
    tokens = out_grads.shape[0]
    width = BLK
    own_blocks = block_ids.shape[1]
    blocks_per = out_grads.shape[1] // width
    model_width = activations.shape[1] * shards
    inv_block = 1.0 / math.sqrt(width)
    inv_shard = 1.0 / math.sqrt(shards)
    partial_gram = jnp.dot(activations, activations.T, preferred_element_type=jnp.float32)
    token_gram = lax.psum(partial_gram, "shard").astype(jnp.bfloat16)
    sign_values = (1 - 2 * sign_bits).astype(jnp.bfloat16)
    flipped = (out_grads * sign_values[None, :]).reshape(tokens, blocks_per, width)
    block_table = parity_table(width).astype(jnp.bfloat16)
    local_mix = jnp.einsum("tbj,jk->btk", flipped, block_table, preferred_element_type=jnp.float32)
    local_mix = (local_mix * inv_block).astype(jnp.bfloat16)
    running = local_mix.astype(jnp.float32)
    for level in range(shards.bit_length() - 1):
        partner = partner_2(running, "shard", level)
        upper = jnp.right_shift(me_index, level) & 1 == 1
        running = jnp.where(upper, partner - running, running + partner)
    mixed = (running * inv_shard).astype(jnp.bfloat16)
    outgoing, own_sources = route_sampled(
        mixed, block_ids, me_index, shards, blocks_per, tokens, width
    )
    incoming = lax.all_to_all(outgoing, "shard", split_axis=0, concat_axis=0, tiled=True)
    sketched = jnp.take(incoming, own_sources, axis=0).reshape(own_blocks, tokens, width)
    weighted = jnp.einsum(
        "tu,jub->jtb", token_gram, sketched, preferred_element_type=jnp.float32
    ).astype(jnp.bfloat16)
    block_gram = jnp.einsum("jtb,ktc->jbkc", sketched, weighted, preferred_element_type=jnp.float32)
    own_cols = own_blocks * width
    block_gram = block_gram.reshape(own_cols, own_cols)
    summed = lax.psum(block_gram, "dp")
    return summed / (lax.axis_size("dp") * tokens * model_width)


def solution(mesh):
    in_specs = (P("dp", "shard"), P("dp", "shard"), P("shard"), P())
    out_specs = P("shard", None)
    return jax.shard_map(body, mesh=mesh, in_specs=in_specs, out_specs=out_specs, check_vma=False)
```

profile of v0, /device:TPU:0, one launch (start us, length us, event | category | flops | bytes accessed | tf_op | source)
XLA Modules:
  0.0 690.9 jit_solution(8151458818415333310)
XLA Ops:
  6.6 6.0 copy.15
  12.6 0.0 copy-done.1
  12.6 3.3 broadcast_multiply_fusion.1
  15.9 4.3 convert_bitcast_fusion
  20.2 3.1 collective-permute-start
  23.3 158.3 %collective-permute-done = f32[28,512,128]{1,2,0:T(8,128)} collective-permute-done((f32[28,512,128]{1,2,0:T(8,128)}, f32[28,512,128]{1,2,0:T(8,128)}, u32[]{:S(2)}, u32[]{:S(2)}) %collective-permute-start) | collective-permute-done | bytes 7340064 | tf_op jit(solution)/shard_map/ppermute | solution.py:12
  181.6 10.6 %add_select_fusion = f32[28,512,128]{1,2,0:T(8,128)} fusion(f32[28,512,128]{1,2,0:T(8,128)} %convert_bitcast_fusion, f32[28,512,128]{1,2,0:T(8,128)} %collective-permute-done, pred[]{:T(512)S(6)} %eq.19), kind=kLoop, calls=%fused_computation.4 | loop fusion | flops 5505024 | bytes 22020096 | tf_op jit(solution)/shard_map/jit(_where)/select_n | solution.py:57
  192.1 2.8 collective-permute-start.1
  194.9 0.1 slice.3
  195.0 0.1 copy.13
  195.1 0.1 fusion.32
  195.2 0.1 copy.12
  195.3 0.1 copy.17
  195.4 0.1 reshape.154
  195.5 0.1 copy.14
  195.7 0.1 broadcast_in_dim.63
  195.7 0.1 broadcast_in_dim.64
  195.8 314.0 %collective-permute-done.1 = f32[28,512,128]{1,2,0:T(8,128)} collective-permute-done((f32[28,512,128]{1,2,0:T(8,128)}, f32[28,512,128]{1,2,0:T(8,128)}, u32[]{:S(2)}, u32[]{:S(2)}) %collective-permute-start.1) | collective-permute-done | bytes 7340064 | tf_op jit(solution)/shard_map/ppermute | solution.py:12
  509.8 9.1 %multiply_convert_fusion = bf16[28,512,128]{1,2,0:T(8,128)(2,1)} fusion(f32[28,512,128]{1,2,0:T(8,128)} %add_select_fusion, f32[28,512,128]{1,2,0:T(8,128)} %collective-permute-done.1, pred[]{:T(512)S(6)} %eq.18), kind=kLoop, calls=%fused_computation.3 | loop fusion | flops 9175040 | bytes 18350080 | tf_op jit(solution)/shard_map/convert_element_type | solution.py:58
  518.9 2.6 gather_fusion
  521.5 1.1 select_multiply_fusion
  522.7 4.6 all-to-all-start
  527.3 0.7 fusion.33
  528.1 63.9 %all-reduce.4 = bf16[512,512]{1,0:T(8,128)(2,1)} all-reduce(f32[512,512]{1,0:T(8,128)S(1)} %fusion.33), channel_id=1, replica_groups=mesh['dp'=8,'shard'=4] {'shard'}, use_global_device_ids=true, to_apply=%region_2.3 | all-reduce | flops 262144 | bytes 1572864 | tf_op jit(solution)/shard_map/psum | solution.py:47
  591.9 0.0 all-to-all-done
  591.9 0.6 gather_fusion.1
  592.6 0.2 bitcast_select_fusion
  592.7 1.8 convolution_convert_fusion
  594.5 3.3 fusion.34
  597.8 0.0 all-reduce.3.cloned.1.call-update
  597.8 81.2 %all-reduce.3.cloned.1.call-done = f32[1024,1024]{1,0:T(8,128)} async-done(((f32[1024,1024]{1,0:T(8,128)}), f32[1024,1024]{1,0:T(8,128)}) %all-reduce.3.cloned.1.call-update) | async-done | bytes 4194320 | tf_op jit(solution)/shard_map/psum | solution.py:70
  679.0 5.0 broadcast_multiply_fusion
  (20 shorter events, 0.1 us)
Async XLA Ops:
  6.5 520.8 %copy-start = (bf16[512,1024]{1,0:T(8,128)(2,1)S(1)}, bf16[512,1024]{1,0:T(8,128)(2,1)}, u32[]{:S(2)}) copy-start(bf16[512,1024]{1,0:T(8,128)(2,1)} %param.4) | copy-start | bytes 3145732
  6.5 6.0 copy-start.1
  20.2 161.4 %collective-permute-start = (f32[28,512,128]{1,2,0:T(8,128)}, f32[28,512,128]{1,2,0:T(8,128)}, u32[]{:S(2)}, u32[]{:S(2)}) collective-permute-start(f32[28,512,128]{1,2,0:T(8,128)} %convert_bitcast_fusion), channel_id=1, source_target_pairs={{0,1},{1,0},{2,3},{3,2},{4,5},{5,4},{6,7},{7,6},{8,9},{9,8},{10,11... | collective-permute-start | bytes 22020104 | tf_op jit(solution)/shard_map/ppermute | solution.py:12
  23.3 171.6 %copy-start.2 = (s32[4,8]{1,0:T(4,128)S(1)}, s32[4,8]{1,0:T(4,128)}, u32[]{:S(2)}) copy-start(s32[4,8]{1,0:T(4,128)} %param.7) | copy-start | bytes 388
  192.1 317.7 %collective-permute-start.1 = (f32[28,512,128]{1,2,0:T(8,128)}, f32[28,512,128]{1,2,0:T(8,128)}, u32[]{:S(2)}, u32[]{:S(2)}) collective-permute-start(f32[28,512,128]{1,2,0:T(8,128)} %add_select_fusion), channel_id=1, source_target_pairs={{0,2},{1,3},{2,0},{3,1},{4,6},{5,7},{6,4},{7,5},{8,10},{9,11},{10,... | collective-permute-start | bytes 22020104 | tf_op jit(solution)/shard_map/ppermute | solution.py:12
  522.7 69.3 %all-to-all-start = ((bf16[4,2,512,128]{2,3,1,0:T(8,128)(2,1)}), bf16[4,2,512,128]{2,3,1,0:T(8,128)(2,1)S(1)}, u32[]{:S(2)}, u32[]{:S(2)}) async-start(bf16[4,2,512,128]{2,3,1,0:T(8,128)(2,1)} %select_multiply_fusion), calls=%async_computation | async-start | bytes 2097152 | tf_op jit(solution)/shard_map/all_to_all | solution.py:62
  527.3 151.7 %all-reduce.3.cloned.1.call-start = ((), (), s32[]{:S(2)}) async-start(), calls=%async_computation.1 | async-start | bytes 8388608 | tf_op jit(solution)/shard_map/psum | solution.py:70
Sparse Core Ops, SparseCore 0:
  598.0 80.9 all-reduce.2
where the time goes:
time: 691 us
  waiting for transfers between devices  553 us (80%)
  blocking collectives  63.9 us (9%)
  other arithmetic  29.5 us (4%)
  between operations  13.5 us (2%)
  starting transfers between devices  10.5 us (2%)
  matrix products  10.1 us (1%)
  local copies, waits for them, and re-layouts  10 us (1%)
    ppermute x2, waiting for transfers between devices, partner_2(): lax.ppermute(x, axis, [(i, i ^ 1 << distance) for i in range(lax.axis_siz...  472 us
    psum x1, waiting for transfers between devices, body(): summed = lax.psum(block_gram, 'dp')  81.2 us
    psum x1, blocking collectives, body(): token_gram = lax.psum(partial_gram, 'shard').astype(jnp.bfloat16)  63.9 us
  transfers between devices with their start and end apart: 4, of which 3 were waited for; matrix products, arithmetic and copies ran while one was open for 0% of the time, Pallas kernels for 0%

commit v1 on v0

--- a/solution.py
+++ b/solution.py
@@ -1,3 +1,4 @@
+import functools
 import math
 import jax
 import jax.numpy as jnp
@@ -6,6 +7,21 @@
 
 BLK = 128
 CAP = 2
+
+
+def post_leaves(mat, ax_name):
+    n_peers_all = jax.lax.axis_size(ax_name)
+    long_array = mat
+    for b in [dev_j for dev_j in (1, 2, 4, 8, 16) if dev_j < n_peers_all]:
+        side_arr = range(n_peers_all)
+        response = map(lambda dev: (dev, dev ^ b), side_arr)
+        y2 = list(response)
+        t1 = jax.lax.ppermute(long_array, ax_name, y2)
+        long_array = long_array + t1
+    return long_array
+
+
+resolve_boxes_by_axis = functools.partial(post_leaves, ax_name="dp")
 
 
 def partner_2(x, axis, distance):
@@ -67,7 +83,7 @@
     block_gram = jnp.einsum("jtb,ktc->jbkc", sketched, weighted, preferred_element_type=jnp.float32)
     own_cols = own_blocks * width
     block_gram = block_gram.reshape(own_cols, own_cols)
-    summed = lax.psum(block_gram, "dp")
+    summed = resolve_boxes_by_axis(block_gram)
     return summed / (lax.axis_size("dp") * tokens * model_width)
 
 

time: 691 us -> 787 us (1.14)
  waiting for transfers between devices: 553 us -> 661 us
  between operations: 13.5 us -> 0.14 us
    ppermute x0 -> x3, waiting for transfers between devices: none -> 189 us  [post_leaves(): t1 = jax.lax.ppermute(long_array, ax_name, y2)]
    psum x1 -> x0, waiting for transfers between devices: 81.2 us -> none  [body(): summed = lax.psum(block_gram, 'dp')]
  transfers between devices with their start and end apart: 4 -> 6, of which waited for: 3 -> 5; matrix products, arithmetic and copies ran while one was open for 0% -> 0% of each run, Pallas kernels for 0% -> 0%
where the time goes in v1:
time: 787 us
  waiting for transfers between devices  661 us (84%)
  blocking collectives  63.8 us (8%)
  other arithmetic  30.2 us (4%)
  starting transfers between devices  13.6 us (2%)
  local copies, waits for them, and re-layouts  10 us (1%)
  matrix products  8.07 us (1%)
    ppermute x2, waiting for transfers between devices, partner_2(): lax.ppermute(x, axis, [(i, i ^ 1 << distance) for i in range(lax.axis_siz...  472 us
    ppermute x3, waiting for transfers between devices, post_leaves(): t1 = jax.lax.ppermute(long_array, ax_name, y2)  189 us
    psum x1, blocking collectives, body(): token_gram = lax.psum(partial_gram, 'shard').astype(jnp.bfloat16)  63.8 us
  transfers between devices with their start and end apart: 6, of which 5 were waited for; matrix products, arithmetic and copies ran while one was open for 0% of the time, Pallas kernels for 0%

profile of v1, /device:TPU:0, one launch (start us, length us, event | category | flops | bytes accessed | tf_op | source)
XLA Modules:
  0.0 786.7 jit_solution(17703151579495159882)
XLA Ops:
  0.0 6.0 copy.15
  6.1 3.3 broadcast_multiply_fusion
  9.4 4.3 convert_bitcast_fusion
  13.7 3.1 collective-permute-start
  16.7 158.3 %collective-permute-done = f32[28,512,128]{1,2,0:T(8,128)} collective-permute-done((f32[28,512,128]{1,2,0:T(8,128)}, f32[28,512,128]{1,2,0:T(8,128)}, u32[]{:S(2)}, u32[]{:S(2)}) %collective-permute-start) | collective-permute-done | bytes 7340064 | tf_op jit(solution)/shard_map/ppermute | solution.py:28
  175.0 10.6 %add_select_fusion = f32[28,512,128]{1,2,0:T(8,128)} fusion(f32[28,512,128]{1,2,0:T(8,128)} %convert_bitcast_fusion, f32[28,512,128]{1,2,0:T(8,128)} %collective-permute-done, pred[]{:T(512)S(6)} %eq.19), kind=kLoop, calls=%fused_computation.4 | loop fusion | flops 5505024 | bytes 22020096 | tf_op jit(solution)/shard_map/jit(_where)/select_n | solution.py:73
  185.6 2.8 collective-permute-start.1
  188.4 0.1 slice.3
  188.5 0.1 fusion.32
  188.7 0.1 copy.12
  188.8 0.1 copy.17
  189.0 0.1 copy.14
  189.2 0.1 broadcast_in_dim.64
  189.3 313.9 %collective-permute-done.1 = f32[28,512,128]{1,2,0:T(8,128)} collective-permute-done((f32[28,512,128]{1,2,0:T(8,128)}, f32[28,512,128]{1,2,0:T(8,128)}, u32[]{:S(2)}, u32[]{:S(2)}) %collective-permute-start.1) | collective-permute-done | bytes 7340064 | tf_op jit(solution)/shard_map/ppermute | solution.py:28
  503.3 9.1 %multiply_convert_fusion = bf16[28,512,128]{1,2,0:T(8,128)(2,1)} fusion(f32[28,512,128]{1,2,0:T(8,128)} %add_select_fusion, f32[28,512,128]{1,2,0:T(8,128)} %collective-permute-done.1, pred[]{:T(512)S(6)} %eq.18), kind=kLoop, calls=%fused_computation.3 | loop fusion | flops 9175040 | bytes 18350080 | tf_op jit(solution)/shard_map/convert_element_type | solution.py:74
  512.3 2.6 gather_fusion
  515.0 1.1 select_multiply_fusion
  516.1 4.7 all-to-all-start
  520.8 0.7 fusion.33
  521.6 63.8 %all-reduce.1 = bf16[512,512]{1,0:T(8,128)(2,1)} all-reduce(f32[512,512]{1,0:T(8,128)S(1)} %fusion.33), channel_id=1, replica_groups=mesh['dp'=8,'shard'=4] {'shard'}, use_global_device_ids=true, to_apply=%region_2.3 | all-reduce | flops 262144 | bytes 1572864 | tf_op jit(solution)/shard_map/psum | solution.py:63
  585.4 0.6 gather_fusion.1
  586.0 0.2 bitcast_select_fusion
  586.2 1.8 convolution_convert_fusion
  588.0 1.3 fusion.34
  589.4 7.1 collective-permute-done.2
  596.5 1.4 add.98
  597.9 1.5 collective-permute-start.3
  599.4 91.2 %collective-permute-done.3 = f32[1024,1024]{1,0:T(8,128)S(1)} collective-permute-done((f32[1024,1024]{1,0:T(8,128)S(1)}, f32[1024,1024]{1,0:T(8,128)S(1)}, u32[]{:S(2)}, u32[]{:S(2)}) %collective-permute-start.3) | collective-permute-done | bytes 4194336 | tf_op jit(solution)/shard_map/ppermute | solution.py:19
  690.5 1.4 add.99
  691.9 1.6 collective-permute-start.4
  693.5 90.3 %collective-permute-done.4 = f32[1024,1024]{1,0:T(8,128)S(1)} collective-permute-done((f32[1024,1024]{1,0:T(8,128)S(1)}, f32[1024,1024]{1,0:T(8,128)S(1)}, u32[]{:S(2)}, u32[]{:S(2)}) %collective-permute-start.4) | collective-permute-done | bytes 4194336 | tf_op jit(solution)/shard_map/ppermute | solution.py:19
  783.7 3.0 add_multiply_fusion
  (25 shorter events, 0.4 us)
Async XLA Ops:
  0.0 520.8 %copy-start = (bf16[512,1024]{1,0:T(8,128)(2,1)S(1)}, bf16[512,1024]{1,0:T(8,128)(2,1)}, u32[]{:S(2)}) copy-start(bf16[512,1024]{1,0:T(8,128)(2,1)} %param.4) | copy-start | bytes 3145732
  0.0 6.0 copy-start.1
  13.7 161.4 %collective-permute-start = (f32[28,512,128]{1,2,0:T(8,128)}, f32[28,512,128]{1,2,0:T(8,128)}, u32[]{:S(2)}, u32[]{:S(2)}) collective-permute-start(f32[28,512,128]{1,2,0:T(8,128)} %convert_bitcast_fusion), channel_id=1, source_target_pairs={{0,1},{1,0},{2,3},{3,2},{4,5},{5,4},{6,7},{7,6},{8,9},{9,8},{10,11... | collective-permute-start | bytes 22020104 | tf_op jit(solution)/shard_map/ppermute | solution.py:28
  16.7 171.6 %copy-start.2 = (s32[4,8]{1,0:T(4,128)S(1)}, s32[4,8]{1,0:T(4,128)}, u32[]{:S(2)}) copy-start(s32[4,8]{1,0:T(4,128)} %param.7) | copy-start | bytes 388
  185.6 317.7 %collective-permute-start.1 = (f32[28,512,128]{1,2,0:T(8,128)}, f32[28,512,128]{1,2,0:T(8,128)}, u32[]{:S(2)}, u32[]{:S(2)}) collective-permute-start(f32[28,512,128]{1,2,0:T(8,128)} %add_select_fusion), channel_id=1, source_target_pairs={{0,2},{1,3},{2,0},{3,1},{4,6},{5,7},{6,4},{7,5},{8,10},{9,11},{10,... | collective-permute-start | bytes 22020104 | tf_op jit(solution)/shard_map/ppermute | solution.py:28
  516.1 69.3 %all-to-all-start = ((bf16[4,2,512,128]{2,3,1,0:T(8,128)(2,1)}), bf16[4,2,512,128]{2,3,1,0:T(8,128)(2,1)S(1)}, u32[]{:S(2)}, u32[]{:S(2)}) async-start(bf16[4,2,512,128]{2,3,1,0:T(8,128)(2,1)} %select_multiply_fusion), calls=%async_computation | async-start | bytes 2097152 | tf_op jit(solution)/shard_map/all_to_all | solution.py:78
  589.3 7.2 collective-permute-start.2
  597.9 92.7 %collective-permute-start.3 = (f32[1024,1024]{1,0:T(8,128)S(1)}, f32[1024,1024]{1,0:T(8,128)S(1)}, u32[]{:S(2)}, u32[]{:S(2)}) collective-permute-start(f32[1024,1024]{1,0:T(8,128)S(1)} %add.98), channel_id=1, source_target_pairs={{0,8},{4,12},{8,0},{12,4},{16,24},{20,28},{24,16},{28,20},{1,9},{5... | collective-permute-start | bytes 12582920 | tf_op jit(solution)/shard_map/ppermute | solution.py:19
  691.9 91.8 %collective-permute-start.4 = (f32[1024,1024]{1,0:T(8,128)S(1)}, f32[1024,1024]{1,0:T(8,128)S(1)}, u32[]{:S(2)}, u32[]{:S(2)}) collective-permute-start(f32[1024,1024]{1,0:T(8,128)S(1)} %add.99), channel_id=1, source_target_pairs={{0,16},{4,20},{8,24},{12,28},{16,0},{20,4},{24,8},{28,12},{1,17},{... | collective-permute-start | bytes 12582920 | tf_op jit(solution)/shard_map/ppermute | solution.py:19
